TPU v7x, 768 devices: a whole 4x8x12 slice. The times are simulated.
768 devices in a mesh: wave: 24 (over z, core), lev: 32 (over y, x).
Axes of the slice: x: 4, y: 8, z: 12, core: 2. Of those that a mesh axis runs over, the one named last changes fastest.
Arguments:
- spectral: bfloat16 [1296, 2, 3, 32, 1296], P('wave', None, None, 'lev'), may hold values from -6 to 6
- legendre: bfloat16 [1296, 24, 1296], P('wave'), may hold values from -0.15625 to 0.15625
- gauss: float32 [48], replicated, may hold values from 0.2 to 2
- wave_order: int32 [1296], replicated, may hold values from 0 to 1295, each once
- pair_order: int32 [24], replicated, may hold values from 0 to 23, each once
- nlon: int32 [24], replicated, may hold values from 4 to 4096, as said below
Outputs:
- grid: float32 [48, 3, 32, 4096], P('wave', None, None, 'lev')
- tendency: bfloat16 [1296, 2, 3, 32, 1296], P('wave', None, None, 'lev')
Inputs may be any that keep to these rules, and one draw needn't show every extreme that they name: `wave_order`: each wavenumber is held by exactly one row. `pair_order`: each latitude pair is held by exactly one pair row. `nlon`: every count is a multiple of 4, and some pair has exactly 4096 points.
All inputs are finite; a program needn't handle non-finite values.
Results may differ from a plain program's by a relative error of at most 0.0074.
Values may be sent and summed in bfloat16 or wider, within the bound.
A program may use at most 128 MiB of HBM per device.

v0:
```python
import math

import jax
import jax.numpy as jnp
from jax import lax
from jax.sharding import PartitionSpec as P


def unit_circle(longitude, wavenumbers, points):
    product = longitude[:, None] * wavenumbers[None, :]
    turns = jnp.round(product / points)
    angles = (product - turns * points) * (2.0 * math.pi / points)
    return jnp.cos(angles), jnp.sin(angles)


def two_terms(x):
    high = x.astype(jnp.bfloat16)
    low = (x - high.astype(jnp.float32)).astype(jnp.bfloat16)
    return high, low


def local(spectral, legendre, gauss, wave_order, pair_order, nlon):
    rows, _, fields, _, modes = spectral.shape
    pairs = legendre.shape[1]
    levels = lax.axis_size("lev")
    wave_me = lax.axis_index("wave")
    lev_me = lax.axis_index("lev")
    columns = 2 * fields
    seg = 128
    bf16 = jnp.bfloat16
    f32 = jnp.float32
    highest = lax.Precision.HIGHEST
    own_modes = lax.dynamic_slice_in_dim(wave_order, wave_me * rows, rows)
    degree = lax.iota(jnp.int32, modes)
    upper = degree[None, :] >= own_modes[:, None]
    even = (degree[None, :] + own_modes[:, None]) % 2 == 0
    keep_north = upper.astype(bf16)
    keep_south = jnp.where(upper, jnp.where(even, 1.0, -1.0), 0.0).astype(bf16)
    flat = spectral.reshape(rows, columns, modes)
    both = jnp.concatenate([flat * keep_north[:, None, :], flat * keep_south[:, None, :]], axis=1)
    folded = jnp.einsum("ojb,oub->ujo", both, legendre, preferred_element_type=f32)
    pair_ids = lax.iota(jnp.int32, pairs)
    picker = (pair_order[:, None] == pair_ids[None, :]).astype(bf16)
    ordered = jnp.einsum(
        "ip,pcr->icr", picker, folded.astype(bf16), preferred_element_type=f32
    ).astype(bf16)
    received = lax.all_to_all(ordered, "wave", split_axis=0, concat_axis=2, tiled=True)
    coefficients = received.reshape(2, 2, fields, modes).astype(f32)
    my_pair = lax.dynamic_index_in_dim(pair_order, wave_me, 0, keepdims=False)
    points_int = jnp.sum(jnp.where(pair_ids == my_pair, nlon, 0))
    points = points_int.astype(f32)
    my_gauss = lax.dynamic_slice_in_dim(gauss, 2 * my_pair, 2)
    orders = wave_order.astype(f32)
    near_cos, near_sin = unit_circle(lax.iota(f32, seg), orders, points)
    far_cos, far_sin = unit_circle(lax.iota(f32, levels) * float(seg), orders, points)
    inside = (2 * wave_order < points_int).astype(f32)
    real = (coefficients[:, 0] * inside)[:, :, None, :]
    imag = (coefficients[:, 1] * inside)[:, :, None, :]
    turned_real = real * near_cos - imag * near_sin
    turned_imag = real * near_sin + imag * near_cos
    turned = jnp.stack([turned_real, turned_imag], axis=0).astype(bf16)
    far = jnp.stack([far_cos, -far_sin], axis=1)
    high, low = two_terms(far)
    far_terms = jnp.concatenate([high, low], axis=0)
    sums = jnp.einsum("acm,chfbm->ahfb", far_terms, turned, preferred_element_type=f32)
    sums = sums[:levels] + sums[levels:]
    longitude = (
        seg * lax.iota(jnp.int32, levels)[:, None] + lax.iota(jnp.int32, seg)[None, :]
    )
    scale = jnp.where(longitude < points_int, 1.0 / math.sqrt(modes), 0.0)
    by_segment = sums * scale[:, None, None, :]
    by_level = lax.all_to_all(by_segment, "lev", split_axis=0, concat_axis=0, tiled=True)
    pieces = jnp.moveaxis(by_level, 0, 2)
    east = pieces[:, 0]
    north = pieces[:, 1]
    heat = pieces[:, 2]
    level_ids = lax.iota(jnp.int32, levels)
    above = (level_ids[None, :] >= level_ids[:, None]).astype(f32)
    geopotential = jnp.einsum("el,slo->seo", above, heat, precision=highest) * (
        1.0 / math.sqrt(levels)
    )
    fluxes = jnp.stack(
        [east * heat, north * heat, east * north + geopotential], axis=1
    ).astype(bf16)
    back = lax.all_to_all(fluxes, "lev", split_axis=2, concat_axis=2, tiled=True)
    inner = jnp.einsum("hfab,acm->chfbm", back, far.astype(bf16), preferred_element_type=f32)
    inner_low = jnp.einsum("hfab,acm->chfbm", back, low, preferred_element_type=f32)
    inner = inner + inner_low
    gathered_cos = inner[0]
    gathered_sin = -inner[1]
    sum_real = jnp.sum(gathered_cos * near_cos - gathered_sin * near_sin, axis=2)
    sum_imag = -jnp.sum(gathered_cos * near_sin + gathered_sin * near_cos, axis=2)
    factor = (my_gauss / jnp.sqrt(points))[:, None, None, None] * inside
    weighted = (jnp.stack([sum_real, sum_imag], axis=1) * factor).astype(bf16)
    weighted = weighted.reshape(2 * columns, modes)
    returned = lax.all_to_all(
        weighted.reshape(1, 2 * columns, modes), "wave", split_axis=2, concat_axis=0, tiled=True
    )
    natural = jnp.einsum("ip,icr->rcp", picker, returned, preferred_element_type=f32).astype(bf16)
    contracted = jnp.einsum("rcp,rpn->rcn", natural, legendre, preferred_element_type=f32)
    parity = jnp.where(even, 1.0, -1.0).astype(f32)
    outer_scale = upper.astype(f32) * math.sqrt(modes / (2 * pairs))
    combined = (
        contracted[:, :columns] + parity[:, None, :] * contracted[:, columns:]
    ) * outer_scale[:, None, :]
    tendency = combined.astype(bf16).reshape(rows, 2, fields, 1, modes)
    return (pieces, tendency)


def solution(mesh):
    in_specs = (P("wave", None, None, "lev", None), P("wave", None, None), P(), P(), P(), P())
    out_specs = (P("wave", None, None, "lev"), P("wave", None, None, "lev", None))
    return jax.shard_map(local, mesh=mesh, in_specs=in_specs, out_specs=out_specs, check_vma=False)
```

profile of v0, /device:TPU:1, one launch (start us, length us, event | category | flops | bytes accessed | tf_op | source)
XLA Modules:
  0.0 111.6 jit_solution(11503835812852322234)
XLA Ops:
  0.7 0.9 dynamic_slice.11
  1.9 1.3 %copy.45 = bf16[54,2,3,1,1296]{4,0,2,1,3:T(8,128)(2,1)S(1)} copy(bf16[54,2,3,1,1296]{4,1,3,2,0:T(2,128)(2,1)} %param.6) | data formatting | bytes 1679616 | tf_op args[0]
  3.9 1.3 %fusion.15 = bf16[24,12,54]{0,1,2:T(8,128)(2,1)S(1)} fusion(bf16[54,24,1296]{2,1,0:T(8,128)(2,1)S(1)} %copy-done, bf16[54,6,1296]{2,1,0:T(8,128)(2,1)S(1)} %get-tuple-element.15, bf16[54,6,1296]{2,1,0:T(8,128)(2,1)S(1)} %get-tuple-element.14), kind=kOutput, calls=%fused_computation.23 | convolution fusion | flops 43685568 | bytes 5069952 | tf_op jit(solution)/shard_map/ojb,oub->ujo/dot_general | solution.py:41
  5.5 0.8 reshape.377
  6.3 16.7 %all-to-all-start = ((bf16[24,2,324]{2,1,0:T(2,128)(2,1)}), bf16[24,2,324]{2,1,0:T(2,128)(2,1)S(1)}, u32[]{:S(2)}, u32[]{:S(2)}) async-start(bf16[24,2,324]{2,1,0:T(2,128)(2,1)} %reshape.377), calls=%async_computation | async-start | bytes 73728 | tf_op jit(solution)/shard_map/all_to_all | solution.py:47
  23.6 1.3 %fusion.67 = s32[]{:T(128)} fusion(s32[24]{0:T(128)S(1)} %copy-done.4, s32[]{:T(128)} %bitcast), kind=kLoop, calls=%fused_computation.100 | loop fusion | flops 71 | bytes 104 | tf_op jit(solution)/shard_map/reduce_sum | solution.py:50
  25.6 2.5 %fusion.27 = (f32[128,1296]{0,1:T(8,128)S(1)}, f32[128,1296]{0,1:T(8,128)S(1)}) fusion(f32[]{:T(128)S(6)} %div.42, f32[]{:T(128)S(6)} %convert_element_type.82, f32[1296]{0:T(1024)S(1)} %convert_element_type.81), kind=kLoop, calls=%fused_computation.38 | loop fusion | flops 995328 | bytes 1332296 | tf_op jit(solution)/shard_map/cos | solution.py:13
  30.2 2.6 %all-to-all-done = bf16[24,2,324]{2,1,0:T(2,128)(2,1)S(1)} async-done(((bf16[24,2,324]{2,1,0:T(2,128)(2,1)}), bf16[24,2,324]{2,1,0:T(2,128)(2,1)S(1)}, u32[]{:S(2)}, u32[]{:S(2)}) %all-to-all-start) | async-done | bytes 31136 | tf_op jit(solution)/shard_map/all_to_all | solution.py:47
  33.2 2.5 %subtract_convert_fusion = (bf16[1,2,3,128,1296]{3,4,0,2,1:T(8,128)(2,1)S(1)}, bf16[1,2,3,128,1296]{3,4,0,2,1:T(8,128)(2,1)S(1)}) fusion(f32[128,1296]{0,1:T(8,128)S(1)} %get-tuple-element.23, f32[2,3,1296]{2,1,0:T(4,128)S(1)} %get-tuple-element.19, f32[128,1296]{0,1:T(8,128)S(1)} %get-tuple-element.22, f32[2,3,1296]{2,1,0:T(4,128)S(1)} %get-tuple-element.18), kind=kLoop, calls=%fused_computation.11 | loop fusion | flops 7962624 | bytes 5370624 | tf_op jit(solution)/shard_map/convert.7
  35.8 0.8 fusion.18
  37.3 9.7 %all-to-all-start.1 = ((f32[32,2,3,128]{3,1,2,0:T(2,128)}), f32[32,2,3,128]{3,1,2,0:T(2,128)S(1)}, u32[]{:S(2)}, u32[]{:S(2)}) async-start(f32[32,2,3,128]{3,1,2,0:T(2,128)} %copy.53), calls=%async_computation.1 | async-start | bytes 196608 | tf_op jit(solution)/shard_map/all_to_all | solution.py:72
  47.8 8.3 %all-to-all-done.1 = f32[32,2,3,128]{3,1,2,0:T(2,128)S(1)} async-done(((f32[32,2,3,128]{3,1,2,0:T(2,128)}), f32[32,2,3,128]{3,1,2,0:T(2,128)S(1)}, u32[]{:S(2)}, u32[]{:S(2)}) %all-to-all-start.1) | async-done | bytes 98336 | tf_op jit(solution)/shard_map/all_to_all | solution.py:72
  57.0 4.0 %all-to-all-start.2 = ((bf16[2,3,32,128]{3,0,1,2:T(2,128)(2,1)}), bf16[2,3,32,128]{3,0,1,2:T(2,128)(2,1)S(1)}, u32[]{:S(2)}, u32[]{:S(2)}) async-start(bf16[2,3,32,128]{3,0,1,2:T(2,128)(2,1)} %copy.55), calls=%async_computation.2 | async-start | bytes 98304 | tf_op jit(solution)/shard_map/all_to_all | solution.py:85
  61.1 8.5 %all-to-all-done.2 = bf16[2,3,32,128]{3,0,1,2:T(2,128)(2,1)S(1)} async-done(((bf16[2,3,32,128]{3,0,1,2:T(2,128)(2,1)}), bf16[2,3,32,128]{3,0,1,2:T(2,128)(2,1)S(1)}, u32[]{:S(2)}, u32[]{:S(2)}) %all-to-all-start.2) | async-done | bytes 49184 | tf_op jit(solution)/shard_map/all_to_all | solution.py:85
  69.6 1.2 %fusion.43 = f32[2,1296,2,3,128]{4,1,3,2,0:T(8,128)S(1)} fusion(bf16[2,3,32,128]{3,0,1,2:T(2,128)(2,1)S(1)} %all-to-all-done.2, f32[32,1,1296]{2,0,1:T(8,128)S(1)} %get-tuple-element.21, f32[32,1,1296]{2,0,1:T(8,128)S(1)} %get-tuple-element.20), kind=kOutput, calls=%fused_computation.62 | convolution fusion | flops 127733760 | bytes 8343552 | tf_op jit(solution)/shard_map/hfab,acm->chfbm/dot_general | solution.py:86
  70.8 1.3 %add_bitcast_fusion = f32[2,2,3,128,1296]{3,4,2,1,0:T(8,128)S(1)} fusion(f32[2,1296,2,3,128]{4,1,3,2,0:T(8,128)S(1)} %fusion.43, bf16[32,2,1296]{2,0,1:T(8,128)(2,1)S(1)} %subtract_convert_fusion.1, bf16[2,3,32,128]{3,0,1,2:T(2,128)(2,1)S(1)} %all-to-all-done.2), kind=kOutput, calls=%fused_computation | convolution fusion | flops 129392640 | bytes 16140288 | tf_op jit(solution)/shard_map/hfab,acm->chfbm/dot_general | solution.py:87
  72.1 2.9 %subtract_reduce_fusion = (f32[2,3,1296]{2,1,0:T(4,128)S(1)}, f32[2,3,1296]{2,1,0:T(4,128)S(1)}) fusion(f32[2,2,3,128,1296]{3,4,2,1,0:T(8,128)S(1)} %add_bitcast_fusion, f32[128,1296]{0,1:T(8,128)S(1)} %get-tuple-element.23, f32[128,1296]{0,1:T(8,128)S(1)} %get-tuple-element.22), kind=kLoop, calls=%fused_computation.9 | loop fusion | flops 8942400 | bytes 9351936 | tf_op jit(solution)/shard_map/reduce_sum | solution.py:91
  75.1 1.0 copy.58
  76.7 7.5 %reduce = bf16[1296,12]{1,0:T(8,128)(2,1)S(1)} reduce(bf16[1296,1,12]{2,1,0:T(2,128)(2,1)S(1)} %bitcast.106, bf16[]{:T(256)} %broadcast.377), dimensions={1}, to_apply=%bitcast.97.reduce_sub_computation | reduce | bytes 62210
  84.2 1.0 reshape.379
  85.2 9.7 %all-to-all-start.3 = ((bf16[24,2,324]{2,1,0:T(2,128)(2,1)}), bf16[24,2,324]{2,1,0:T(2,128)(2,1)S(1)}, u32[]{:S(2)}, u32[]{:S(2)}) async-start(bf16[24,2,324]{2,1,0:T(2,128)(2,1)} %reshape.379), calls=%async_computation.3 | async-start | bytes 73728 | tf_op jit(solution)/shard_map/all_to_all | solution.py:96
  95.5 9.2 %all-to-all-done.3 = bf16[24,2,324]{2,1,0:T(2,128)(2,1)S(1)} async-done(((bf16[24,2,324]{2,1,0:T(2,128)(2,1)}), bf16[24,2,324]{2,1,0:T(2,128)(2,1)S(1)}, u32[]{:S(2)}, u32[]{:S(2)}) %all-to-all-start.3) | async-done | bytes 31136 | tf_op jit(solution)/shard_map/all_to_all | solution.py:96
  106.5 2.9 %fusion.71 = f32[54,12,1296]{2,1,0:T(8,128)S(1)} fusion(bf16[54,12,24]{2,1,0:T(8,128)(2,1)S(1)} %copy.60, bf16[54,24,1296]{2,1,0:T(8,128)(2,1)} %param.7), kind=kOutput, calls=%fused_computation.106 | convolution fusion | flops 40310784 | bytes 6749568 | tf_op jit(solution)/shard_map/rcp,rpn->rcn/dot_general | solution.py:100
  110.0 1.6 %copy.63 = bf16[54,2,3,1,1296]{4,1,3,2,0:T(2,128)(2,1)} copy(bf16[54,2,3,1,1296]{4,0,2,1,3:T(8,128)(2,1)S(1)} %bitcast.105) | data formatting | bytes 1679616
  (50 shorter events, 9.7 us)
Async XLA Ops:
  0.6 3.2 %copy-start = (bf16[54,24,1296]{2,1,0:T(8,128)(2,1)S(1)}, bf16[54,24,1296]{2,1,0:T(8,128)(2,1)}, u32[]{:S(2)}) copy-start(bf16[54,24,1296]{2,1,0:T(8,128)(2,1)} %param.7) | copy-start | bytes 10077700
  3.8 1.4 %copy-start.2 = (s32[24]{0:T(128)S(1)}, s32[24]{0:T(128)}, u32[]{:S(2)}) copy-start(s32[24]{0:T(128)} %param.10) | copy-start | bytes 292
  3.8 19.2 %copy-start.1 = (s32[1296]{0:T(1024)S(1)}, s32[1296]{0:T(1024)}, u32[]{:S(2)}) copy-start(s32[1296]{0:T(1024)} %param.9) | copy-start | bytes 15556
  3.8 19.8 %copy-start.4 = (s32[24]{0:T(128)S(1)}, s32[24]{0:T(128)}, u32[]{:S(2)}) copy-start(s32[24]{0:T(128)} %param.11) | copy-start | bytes 292
  6.3 26.6 %all-to-all-start = ((bf16[24,2,324]{2,1,0:T(2,128)(2,1)}), bf16[24,2,324]{2,1,0:T(2,128)(2,1)S(1)}, u32[]{:S(2)}, u32[]{:S(2)}) async-start(bf16[24,2,324]{2,1,0:T(2,128)(2,1)} %reshape.377), calls=%async_computation | async-start | bytes 73728 | tf_op jit(solution)/shard_map/all_to_all | solution.py:47
  35.8 11.9 %copy-start.3 = (f32[48]{0:T(128)S(1)}, f32[48]{0:T(128)}, u32[]{:S(2)}) copy-start(f32[48]{0:T(128)} %param.8) | copy-start | bytes 580
  37.3 18.8 %all-to-all-start.1 = ((f32[32,2,3,128]{3,1,2,0:T(2,128)}), f32[32,2,3,128]{3,1,2,0:T(2,128)S(1)}, u32[]{:S(2)}, u32[]{:S(2)}) async-start(f32[32,2,3,128]{3,1,2,0:T(2,128)} %copy.53), calls=%async_computation.1 | async-start | bytes 196608 | tf_op jit(solution)/shard_map/all_to_all | solution.py:72
  57.0 12.6 %all-to-all-start.2 = ((bf16[2,3,32,128]{3,0,1,2:T(2,128)(2,1)}), bf16[2,3,32,128]{3,0,1,2:T(2,128)(2,1)S(1)}, u32[]{:S(2)}, u32[]{:S(2)}) async-start(bf16[2,3,32,128]{3,0,1,2:T(2,128)(2,1)} %copy.55), calls=%async_computation.2 | async-start | bytes 98304 | tf_op jit(solution)/shard_map/all_to_all | solution.py:85
  85.2 19.5 %all-to-all-start.3 = ((bf16[24,2,324]{2,1,0:T(2,128)(2,1)}), bf16[24,2,324]{2,1,0:T(2,128)(2,1)S(1)}, u32[]{:S(2)}, u32[]{:S(2)}) async-start(bf16[24,2,324]{2,1,0:T(2,128)(2,1)} %reshape.379), calls=%async_computation.3 | async-start | bytes 73728 | tf_op jit(solution)/shard_map/all_to_all | solution.py:96
where the time goes:
time: 112 us
  starting transfers between devices  40 us (36%)
  waiting for transfers between devices  28.6 us (26%)
  other arithmetic  20.7 us (18%)
  local copies, waits for them, and re-layouts  11.9 us (11%)
  matrix products  8.09 us (7%)
  between operations  2.37 us (2%)
    all_to_all x1, starting transfers between devices, local(): lax.all_to_all(ordered, 'wave', split_axis=0, concat_axis=2, tiled=True)  16.7 us
    all_to_all x1, starting transfers between devices, local(): lax.all_to_all(by_segment, 'lev', split_axis=0, concat_axis=0, tiled=True)  9.67 us
    all_to_all x1, starting transfers between devices, local(): lax.all_to_all(weighted.reshape(1, 2 * columns, modes), 'wave', split_axi...  9.65 us
    all_to_all x1, waiting for transfers between devices, local(): lax.all_to_all(weighted.reshape(1, 2 * columns, modes), 'wave', split_axi...  9.21 us
    all_to_all x1, waiting for transfers between devices, local(): lax.all_to_all(fluxes, 'lev', split_axis=2, concat_axis=2, tiled=True)  8.51 us
    all_to_all x1, waiting for transfers between devices, local(): lax.all_to_all(by_segment, 'lev', split_axis=0, concat_axis=0, tiled=True)  8.3 us
    unnamed x1, other arithmetic  7.54 us
    unnamed x17, local copies, waits for them, and re-layouts  5.77 us
  transfers between devices with their start and end apart: 4, of which 4 were waited for; matrix products, arithmetic and copies ran while one was open for 7% of the time, Pallas kernels for 0%

commit v1 on v0

v1 whole, which is shorter than its diff:
```python
import functools
import math

import jax
import jax.numpy as jnp
from jax import lax
from jax.experimental import pallas as pl
from jax.experimental.pallas import tpu as pltpu
from jax.sharding import PartitionSpec as P

BF16 = jnp.bfloat16
F32 = jnp.float32
MESH = pl.DeviceIdType.MESH
SEG = 128
HALF = 64
ROWS_AT_ONCE = 3
SERIES = [(-1.0) ** i * (2.0 * math.pi) ** (2 * i + 1) / math.factorial(2 * i + 1) for i in range(6)]


def sine_of_turns(t):
    square = t * t
    total = jnp.full_like(t, SERIES[-1])
    for factor in SERIES[-2::-1]:
        total = total * square + factor
    return total * t


def unit_circle(product, points, inverse):
    t = (product - jnp.floor(product * inverse + 0.5) * points) * inverse
    folded = jnp.where(t > 0.25, 0.5 - t, jnp.where(t < -0.25, -0.5 - t, t))
    return sine_of_turns(0.25 - jnp.abs(t)), sine_of_turns(folded)


def nt(a, b):
    return lax.dot_general(a, b, (((1,), (1,)), ((), ())), preferred_element_type=F32)


def kernel(
    waves, levels, fields, rows, modes,
    order_smem, pair_smem, nlon_smem, gauss_smem, spec_ref, leg_hbm, lanes_ref,
    grid_ref, tend_ref,
    leg, cube, flat, send_a, recv_a, near_c, near_s, far, turned,
    send_f, recv_f, flat_p, send_p, recv_p, turned_p, total, send_d, recv_d,
    leg_sem, send_sem, recv_sem,
):
    wave = lax.axis_index("wave")
    lev = lax.axis_index("lev")
    chunks = waves // 2
    parts = 2 * fields
    groups = leg_sem.shape[0]
    group_rows = rows // groups

    def leg_copy(g):
        block = pl.ds(g * group_rows, group_rows)
        return pltpu.make_async_copy(leg_hbm.at[block], leg.at[block], leg_sem.at[g])

    for g in range(groups):
        leg_copy(g).start()

    barrier = pltpu.get_barrier_semaphore()

    @pl.loop(1, waves)
    def _(s):
        pl.semaphore_signal(
            barrier, inc=1, device_id={"wave": lax.rem(wave + s, waves)}, device_id_type=MESH
        )

    @pl.loop(1, levels)
    def _(s):
        pl.semaphore_signal(
            barrier, inc=1, device_id={"lev": lax.rem(lev + s, levels)}, device_id_type=MESH
        )

    def exchange(axis, me, count, source, target, index):
        @pl.loop(0, count - 1)
        def _(t):
            step = (t + 1) // 2
            there = lax.rem(me + count // 2 + step * (1 - 2 * (t % 2)) + count, count)
            pltpu.make_async_remote_copy(
                src_ref=source.at[there],
                dst_ref=target.at[me],
                send_sem=send_sem.at[index],
                recv_sem=recv_sem.at[index],
                device_id={axis: there},
                device_id_type=MESH,
            ).start()

        target[me] = source[me]

    def arrived(count, target, index):
        all_but_one = target.at[pl.ds(0, count - 1)]
        pltpu.make_async_copy(all_but_one, all_but_one, recv_sem.at[index]).wait()

    def left(count, source, index):
        all_but_one = source.at[pl.ds(0, count - 1)]
        pltpu.make_async_copy(all_but_one, all_but_one, send_sem.at[index]).wait()

    cube[...] = jnp.zeros_like(cube)
    degree = lax.broadcasted_iota(jnp.int32, (8, modes), 1)
    sign = (1 - 2 * (degree % 2)).astype(F32)

    def forward_row(r):
        order = order_smem[wave * rows + r]
        turn = (1 - 2 * (order % 2)).astype(F32)
        north = jnp.where(degree >= order, spec_ref[r].astype(F32), 0.0)
        south = north * (sign * turn)
        both = jnp.concatenate([north, south], axis=0).astype(BF16)
        sums = nt(both, leg[r])
        cube[pl.ds(pl.multiple_of(r * 8, 8), 8), : sums.shape[1]] = sums[:8]
        cube[pl.ds(pl.multiple_of((HALF + r) * 8, 8), 8), : sums.shape[1]] = sums[8:]

    per_group = group_rows // ROWS_AT_ONCE
    for g in range(groups):
        leg_copy(g).wait()

        @pl.loop(0, per_group)
        def _(i):
            for k in range(ROWS_AT_ONCE):
                forward_row(g * group_rows + i * ROWS_AT_ONCE + k)

    own_row = lax.broadcasted_iota(jnp.int32, (waves, SEG), 0)
    own_lane = lax.broadcasted_iota(jnp.int32, (waves, SEG), 1)
    held = jnp.zeros((waves, SEG), jnp.int32)
    for i in range(waves):
        held = jnp.where(own_row == i, pair_smem[i], held)
    picker = jnp.where(held == own_lane, 1.0, 0.0).astype(BF16)

    for c in range(8):
        if c < parts:
            block = cube[pl.ds(c, 2 * HALF, stride=8), :].astype(BF16)
            flat[pl.ds(c, waves, stride=8), :] = nt(picker, block)
        else:
            flat[pl.ds(c, waves, stride=8), :] = jnp.zeros((waves, SEG), F32)
    send_a[...] = flat[...].reshape(waves, 8, SEG).astype(BF16)

    pl.semaphore_wait(barrier, waves + levels - 2)
    exchange("wave", wave, waves, send_a, recv_a, 0)

    pair = pair_smem[wave]
    count = nlon_smem[pair]
    points = jnp.full((1, SEG), count.astype(F32))
    inverse = 1.0 / points
    near_k = lax.broadcasted_iota(jnp.int32, (SEG, SEG), 0).astype(F32)
    far_k = (SEG * lax.broadcasted_iota(jnp.int32, (levels, SEG), 0)).astype(F32)

    @pl.loop(0, chunks)
    def _(j):
        orders = lanes_ref[pl.ds(j, 1), :]
        cosine, sine = unit_circle(near_k * orders, points, inverse)
        near_c[j] = cosine
        near_s[j] = sine
        cosine, sine = unit_circle(far_k * orders, points, inverse)
        both = jnp.concatenate([cosine, -sine], axis=1)
        high = both.astype(BF16).astype(F32)
        far[j] = jnp.concatenate([high, both - high], axis=0).astype(BF16)

    arrived(waves, recv_a, 0)

    first_half = lax.broadcasted_iota(jnp.int32, (8, SEG), 1) < HALF

    @pl.loop(0, chunks)
    def _(j):
        even = recv_a[2 * j].astype(F32)
        odd = recv_a[2 * j + 1].astype(F32)
        inside = jnp.where(2.0 * lanes_ref[pl.ds(j, 1), :] < points, 1.0, 0.0)
        north = jnp.where(first_half, even, pltpu.roll(odd, HALF, 1)) * inside
        south = jnp.where(first_half, pltpu.roll(even, HALF, 1), odd) * inside
        cosine = near_c[j]
        sine = near_s[j]
        for h, half in enumerate((north, south)):
            for f in range(fields):
                real = half[2 * f : 2 * f + 1]
                imag = half[2 * f + 1 : 2 * f + 2]
                turned[h * fields + f, j, :, :SEG] = (real * cosine - imag * sine).astype(BF16)
                turned[h * fields + f, j, :, SEG:] = (real * sine + imag * cosine).astype(BF16)

    longitude = SEG * lax.broadcasted_iota(
        jnp.int32, (levels, SEG), 0
    ) + lax.broadcasted_iota(jnp.int32, (levels, SEG), 1)
    scale = jnp.where(longitude < count, 1.0 / math.sqrt(modes), 0.0)
    for hf in range(parts):
        sums = nt(turned[hf, 0], far[0])
        for j in range(1, chunks):
            sums = sums + nt(turned[hf, j], far[j])
        sums = sums.T
        flat_p[pl.ds(hf, levels, stride=8), :] = (sums[:levels] + sums[levels:]) * scale
    for c in range(parts, 8):
        flat_p[pl.ds(c, levels, stride=8), :] = jnp.zeros((levels, SEG), F32)
    send_f[...] = flat_p[...].reshape(levels, 8, SEG).astype(send_f.dtype)
    exchange("lev", lev, levels, send_f, recv_f, 1)
    arrived(levels, recv_f, 1)

    flat_p[...] = recv_f[...].astype(F32).reshape(levels * 8, SEG)
    level_row = lax.broadcasted_iota(jnp.int32, (levels, levels), 0)
    level_lane = lax.broadcasted_iota(jnp.int32, (levels, levels), 1)
    above = jnp.where(level_lane >= level_row, 1.0, 0.0)
    products = []
    for h in range(2):
        east, north, heat = (
            flat_p[pl.ds(h * fields + f, levels, stride=8), :] for f in range(fields)
        )
        for f, value in enumerate((east, north, heat)):
            grid_ref[h, f] = value
        geopotential = jnp.dot(
            above, heat, precision=lax.Precision.HIGHEST, preferred_element_type=F32
        ) * (1.0 / math.sqrt(levels))
        products += [east * heat, north * heat, east * north + geopotential]
    for hf, value in enumerate(products):
        flat_p[pl.ds(hf, levels, stride=8), :] = value
    send_p[...] = flat_p[...].reshape(levels, 8, SEG).astype(BF16)
    exchange("lev", lev, levels, send_p, recv_p, 2)
    arrived(levels, recv_p, 2)

    flat_p[...] = recv_p[...].astype(F32).reshape(levels * 8, SEG)
    for hf in range(parts):
        block = flat_p[pl.ds(hf, levels, stride=8), :]
        turned_p[hf] = jnp.concatenate([block, block], axis=0).T.astype(BF16)
    total[...] = jnp.zeros_like(total)

    root = lax.rsqrt(points)
    factors = [root * gauss_smem[2 * pair + h] for h in range(2)]

    @pl.loop(0, chunks)
    def _(j):
        cosine = near_c[j]
        sine = near_s[j]
        for h in range(2):
            for f in range(fields):
                inner = jnp.dot(turned_p[h * fields + f], far[j], preferred_element_type=F32)
                even = inner[:, :SEG]
                odd = inner[:, SEG:]
                real = jnp.sum(even * cosine + odd * sine, axis=0, keepdims=True)
                imag = jnp.sum(odd * cosine - even * sine, axis=0, keepdims=True)
                total[h, 2 * f : 2 * f + 1] = real
                total[h, 2 * f + 1 : 2 * f + 2] = imag
        inside = jnp.where(2.0 * lanes_ref[pl.ds(j, 1), :] < points, 1.0, 0.0)
        north = total[0] * (factors[0] * inside)
        south = total[1] * (factors[1] * inside)
        send_d[2 * j] = jnp.where(first_half, north, pltpu.roll(south, HALF, 1)).astype(BF16)
        send_d[2 * j + 1] = jnp.where(first_half, pltpu.roll(north, HALF, 1), south).astype(BF16)

    exchange("wave", wave, waves, send_d, recv_d, 3)
    arrived(waves, recv_d, 3)

    flat[...] = recv_d[...].astype(F32).reshape(waves * 8, SEG)
    for c in range(parts):
        block = flat[pl.ds(c, waves, stride=8), :].astype(BF16)
        cube[pl.ds(c, 2 * HALF, stride=8), :] = lax.dot_general(
            block, picker, (((0,), (0,)), ((), ())), preferred_element_type=F32
        )
    outer = math.sqrt(modes / (2 * waves))

    @pl.loop(0, rows // ROWS_AT_ONCE)
    def _(i):
        for k in range(ROWS_AT_ONCE):
            r = i * ROWS_AT_ONCE + k
            order = order_smem[wave * rows + r]
            turn = (1 - 2 * (order % 2)).astype(F32)
            north = cube[pl.ds(pl.multiple_of(r * 8, 8), 8), :]
            south = cube[pl.ds(pl.multiple_of((HALF + r) * 8, 8), 8), :]
            both = jnp.concatenate([north, south], axis=0)[:, :waves].astype(BF16)
            sums = jnp.dot(both, leg[r], preferred_element_type=F32)
            mixed = (sums[:8] + sums[8:] * (sign * turn)) * outer
            tend_ref[r] = jnp.where(degree >= order, mixed, 0.0).astype(BF16)

    for index, (size, source) in enumerate(
        ((waves, send_a), (levels, send_f), (levels, send_p), (waves, send_d))
    ):
        left(size, source, index)


def local(spectral, legendre, gauss, wave_order, pair_order, nlon):
    rows, _, fields, _, modes = spectral.shape
    waves = lax.axis_size("wave")
    levels = lax.axis_size("lev")
    parts = 2 * fields
    spec = jnp.transpose(spectral, (0, 2, 3, 1, 4)).reshape(rows, parts, modes)
    spec = jnp.pad(spec, ((0, 0), (0, 8 - parts), (0, 0)))
    lanes = jnp.pad(wave_order.reshape(waves, rows), ((0, 0), (0, HALF - rows)))
    lanes = lanes.reshape(waves // 2, SEG).astype(F32)
    vmem = pl.BlockSpec(memory_space=pltpu.VMEM)
    smem = pl.BlockSpec(memory_space=pltpu.SMEM)
    groups = 3 if rows % (3 * ROWS_AT_ONCE) == 0 else 1
    chunks = waves // 2
    scratch = [
        pltpu.VMEM(legendre.shape, BF16),
        pltpu.VMEM((2 * HALF * 8, SEG), F32),
        pltpu.VMEM((waves * 8, SEG), F32),
        pltpu.VMEM((waves, 8, SEG), BF16),
        pltpu.VMEM((waves, 8, SEG), BF16),
        pltpu.VMEM((chunks, SEG, SEG), F32),
        pltpu.VMEM((chunks, SEG, SEG), F32),
        pltpu.VMEM((chunks, 2 * levels, 2 * SEG), BF16),
        pltpu.VMEM((parts, chunks, SEG, 2 * SEG), BF16),
        pltpu.VMEM((levels, 8, SEG), F32),
        pltpu.VMEM((levels, 8, SEG), F32),
        pltpu.VMEM((levels * 8, SEG), F32),
        pltpu.VMEM((levels, 8, SEG), BF16),
        pltpu.VMEM((levels, 8, SEG), BF16),
        pltpu.VMEM((parts, SEG, 2 * levels), BF16),
        pltpu.VMEM((2, 8, SEG), F32),
        pltpu.VMEM((waves, 8, SEG), BF16),
        pltpu.VMEM((waves, 8, SEG), BF16),
        pltpu.SemaphoreType.DMA((groups,)),
        pltpu.SemaphoreType.DMA((4,)),
        pltpu.SemaphoreType.DMA((4,)),
    ]
    grid, tend = pl.pallas_call(
        functools.partial(kernel, waves, levels, fields, rows, modes),
        out_shape=(
            jax.ShapeDtypeStruct((2, fields, levels, SEG), F32),
            jax.ShapeDtypeStruct((rows, 8, modes), BF16),
        ),
        in_specs=[smem, smem, smem, smem, vmem, pl.BlockSpec(memory_space=pl.ANY), vmem],
        out_specs=(vmem, vmem),
        scratch_shapes=scratch,
        compiler_params=pltpu.CompilerParams(collective_id=0, has_side_effects=True),
    )(wave_order, pair_order, nlon, gauss, spec, legendre, lanes)
    tend = tend[:, :parts].reshape(rows, fields, 1, 2, modes)
    return grid, jnp.transpose(tend, (0, 3, 1, 2, 4))


def solution(mesh):
    in_specs = (P("wave", None, None, "lev", None), P("wave", None, None), P(), P(), P(), P())
    out_specs = (P("wave", None, None, "lev"), P("wave", None, None, "lev", None))
    return jax.shard_map(local, mesh=mesh, in_specs=in_specs, out_specs=out_specs, check_vma=False)
```

time: 112 us -> 68.5 us (0.61)
  Pallas kernels: 0 us -> 59.8 us
  starting transfers between devices: 40 us -> 0 us
  waiting for transfers between devices: 28.6 us -> 0 us
  other arithmetic: 20.7 us -> 0.01 us
  matrix products: 8.09 us -> 0 us
  local copies, waits for them, and re-layouts: 11.9 us -> 7.76 us
  between operations: 2.37 us -> 0.67 us
    pallas_call x0 -> x1, Pallas kernels: none -> 59.8 us  [local(): pl.pallas_call(functools.partial(kernel, waves, levels, fields, rows, mod...]
    all_to_all x4 -> x0, starting transfers between devices: 40 us -> none  [the longest x1 16.7 us: local(): lax.all_to_all(ordered, 'wave', split_axis=0, concat_axis=2, tiled=True)]
    all_to_all x4 -> x0, waiting for transfers between devices: 28.6 us -> none  [the longest x1 9.21 us: local(): lax.all_to_all(weighted.reshape(1, 2 * columns, modes), 'wave', split_axi...]
    dot_general x8 -> x0, matrix products: 8.09 us -> none  [the longest x1 2.89 us: local(): jnp.einsum('rcp,rpn->rcn', natural, legendre, preferred_element_type=f32)]
    unnamed x1 -> x0, other arithmetic: 7.54 us -> none
    reduce_sum x2 -> x0, other arithmetic: 4.25 us -> none  [the longest x1 2.92 us: local(): jnp.sum(gathered_cos * near_cos - gathered_sin * near_sin, axis=2)]
    cos x2 -> x0, other arithmetic: 3.21 us -> none  [unit_circle(): return (jnp.cos(angles), jnp.sin(angles))]
    another operation x3 -> x0, other arithmetic: 2.56 us -> none
  transfers between devices with their start and end apart: 4 -> 0, of which waited for: 4 -> 0; matrix products, arithmetic and copies ran while one was open for 7% -> 0% of each run, Pallas kernels for 0% -> 0%
where the time goes in v1:
time: 68.5 us; the launch traced here: 68.2 us
  Pallas kernels  59.8 us (87%)
  local copies, waits for them, and re-layouts  7.76 us (11%)
    pallas_call x1, Pallas kernels, local(): pl.pallas_call(functools.partial(kernel, waves, levels, fields, rows, mod...  59.8 us
    unnamed x5, local copies, waits for them, and re-layouts  3.54 us
    slice x1, local copies, waits for them, and re-layouts, local(): tend = tend[:, :parts].reshape(rows, fields, 1, 2, modes)  1.38 us

profile of v1, /device:TPU:1, one launch (start us, length us, event | category | flops | bytes accessed | tf_op | source)
XLA Modules:
  0.0 68.2 jit_solution(6949170090736017614)
XLA Ops:
  0.6 0.8 %reshape.16 = s32[24,54]{1,0:T(8,128)S(1)} reshape(s32[1296]{0:T(1024)} %order_smem.1) | data formatting | bytes 10368 | tf_op jit(solution)/shard_map/reshape | solution.py:279
  1.4 0.7 convert_element_type.8.lanes_ref
  2.1 1.3 %copy.9 = bf16[54,2,3,1,1296]{4,0,1,2,3:T(8,128)(2,1)S(1)} copy(bf16[54,2,3,1,1296]{4,1,3,2,0:T(2,128)(2,1)} %param.6) | data formatting | bytes 1679616 | tf_op args[0]
  3.4 0.1 copy.10
  3.5 1.2 %pad.8.spec_ref = bf16[54,8,1296]{2,1,0:T(8,128)(2,1)} pad(bf16[54,6,1296]{2,1,0:T(8,128)(2,1)S(1)} %copy.10, bf16[]{:T(256)} %constant.2.clone.1), padding=0_0x0_2x0_0 | pad | bytes 1959554 | tf_op jit(solution)/shard_map/jit(_pad)/pad | solution.py:278
  4.8 59.8 %shard_map.77 = (f32[2,3,32,128]{3,2,1,0:T(8,128)}, bf16[54,8,1296]{2,1,0:T(8,128)(2,1)}) custom-call(s32[1296]{0:T(1024)} %order_smem.1, s32[24]{0:T(128)} %pair_smem.1, s32[24]{0:T(128)} %nlon_smem.1, f32[48]{0:T(128)} %gauss_smem.1, bf16[54,8,1296]{2,1,0:T(8,128)(2,1)} %pad.8.spec_ref, bf16[54,24,1296]{2,1,0:T(8,128)(2,1)} %leg_hbm.1, ...), custom_call_target="tpu_custom_call" | custom-call | tf_op jit(solution)/shard_map/pallas_call | solution.py:308
  64.5 1.4 %copy.11 = bf16[54,6,1296]{2,0,1:T(8,128)(2,1)S(1)} copy(bf16[54,6,1296]{2,1,0:T(8,128)(2,1)} %bitcast.9) | data formatting | bytes 1679616 | tf_op jit(solution)/shard_map/slice | solution.py:319
  65.9 0.0 copy-start
  65.9 1.6 %copy.12 = bf16[54,2,3,1,1296]{4,1,3,2,0:T(2,128)(2,1)} copy(bf16[54,2,3,1,1296]{4,0,1,2,3:T(8,128)(2,1)S(1)} %bitcast.7) | data formatting | bytes 1679616
  67.5 0.0 copy-done
  67.5 0.6 copy.14
  (1 shorter events, 0.0 us)
Async XLA Ops:
  65.9 1.6 %copy-start = (f32[2,3,32,128]{3,2,1,0:T(8,128)S(1)}, f32[2,3,32,128]{3,2,1,0:T(8,128)}, u32[]{:S(2)}) copy-start(f32[2,3,32,128]{3,2,1,0:T(8,128)} %get-tuple-element.10) | copy-start | bytes 294916

commit v2 on v1

v2 whole, which is shorter than its diff:
```python
import functools
import math

import jax
import jax.numpy as jnp
from jax import lax
from jax.experimental import pallas as pl
from jax.experimental.pallas import tpu as pltpu
from jax.sharding import PartitionSpec as P

BF16 = jnp.bfloat16
F32 = jnp.float32
MESH = pl.DeviceIdType.MESH
SEG = 128
VMEM_LIMIT = 24 * 2**20
HALF = 64
NEAR = 32
ROWS_AT_ONCE = 9
CHUNKS_AT_ONCE = 2
SERIES = [(-1.0) ** i * (2.0 * math.pi) ** (2 * i + 1) / math.factorial(2 * i + 1) for i in range(6)]


def sine_of_turns(t):
    square = t * t
    total = jnp.full_like(t, SERIES[-1])
    for factor in SERIES[-2::-1]:
        total = total * square + factor
    return total * t


def unit_circle(product, points, inverse):
    t = (product - jnp.floor(product * inverse + 0.5) * points) * inverse
    folded = jnp.where(t > 0.25, 0.5 - t, jnp.where(t < -0.25, -0.5 - t, t))
    return sine_of_turns(0.25 - jnp.abs(t)), sine_of_turns(folded)


def nt(a, b):
    return lax.dot_general(a, b, (((1,), (1,)), ((), ())), preferred_element_type=F32)


def one_hot(order, size):
    row = lax.broadcasted_iota(jnp.int32, (size, SEG), 0)
    lane = lax.broadcasted_iota(jnp.int32, (size, SEG), 1)
    held = jnp.zeros((size, SEG), jnp.int32)
    for i in range(size):
        held = jnp.where(row == i, order[i], held)
    return jnp.where(held == lane, 1.0, 0.0).astype(BF16)


def kernel(
    waves, levels, fields, rows, modes,
    order_hbm, pair_hbm, nlon_hbm, gauss_hbm, spec_hbm, leg_hbm,
    grid_ref, recv_d, picker_ref, own_ref,
    order_smem, pair_smem, nlon_smem, gauss_smem, order_row, lanes_ref, spec,
    leg, cube, flat, send_a, recv_a, near_c, near_s, far, turned,
    send_f, recv_f, flat_p, send_p, recv_p, turned_p, total, send_d,
    small_sem, leg_sem, spec_sem, out_sem, send_sem, recv_sem,
):
    wave = lax.axis_index("wave")
    lev = lax.axis_index("lev")
    chunks = waves // 2
    parts = 2 * fields
    groups = leg_sem.shape[0]
    group_rows = rows // groups

    def leg_copy(g):
        block = pl.ds(g * group_rows, group_rows)
        return pltpu.make_async_copy(leg_hbm.at[block], leg.at[block], leg_sem.at[g])

    def spec_copy(g):
        block = pl.ds(g * group_rows, group_rows)
        return pltpu.make_async_copy(spec_hbm.at[block], spec.at[block], spec_sem.at[g])

    small = [
        pltpu.make_async_copy(order_hbm, order_smem, small_sem.at[0]),
        pltpu.make_async_copy(pair_hbm, pair_smem, small_sem.at[1]),
        pltpu.make_async_copy(nlon_hbm, nlon_smem, small_sem.at[2]),
        pltpu.make_async_copy(gauss_hbm, gauss_smem, small_sem.at[3]),
        pltpu.make_async_copy(order_hbm, order_row.at[0], small_sem.at[4]),
    ]
    for copy in small:
        copy.start()
    for g in range(groups):
        spec_copy(g).start()
        leg_copy(g).start()

    barrier = pltpu.get_barrier_semaphore()

    def wrapped(me, step, count):
        return jnp.where(me + step >= count, me + step - count, me + step)

    def far_first(count):
        return sorted(range(1, count), key=lambda s: -min(s, count - s))

    for axis, me, size in (("wave", wave, waves), ("lev", lev, levels)):
        for step in far_first(size):
            pl.semaphore_signal(
                barrier, inc=1, device_id={axis: wrapped(me, step, size)}, device_id_type=MESH
            )

    def exchange(axis, me, count, source, target, index):
        for step in far_first(count):
            there = wrapped(me, step, count)
            pltpu.make_async_remote_copy(
                src_ref=source.at[there],
                dst_ref=target.at[me],
                send_sem=send_sem.at[index],
                recv_sem=recv_sem.at[index],
                device_id={axis: there},
                device_id_type=MESH,
            ).start()

        if index < 3:
            target[me] = source[me]
        else:
            pltpu.make_async_copy(source.at[me], target.at[me], out_sem.at[0]).start()

    def arrived(count, target, index):
        all_but_one = target.at[pl.ds(0, count - 1)]
        pltpu.make_async_copy(all_but_one, all_but_one, recv_sem.at[index]).wait()

    def left(count, source, index):
        all_but_one = source.at[pl.ds(0, count - 1)]
        pltpu.make_async_copy(all_but_one, all_but_one, send_sem.at[index]).wait()

    cube[...] = jnp.zeros_like(cube)
    for copy in small:
        copy.wait()
    degree = lax.broadcasted_iota(jnp.int32, (8, modes), 1)
    padding = jnp.zeros((8 - parts, modes), F32)
    sign = (1 - 2 * (degree % 2)).astype(F32)

    def forward_row(r):
        order = order_smem[wave * rows + r]
        turn = (1 - 2 * (order % 2)).astype(F32)
        north = jnp.where(degree >= order, jnp.concatenate([spec[r].astype(F32).reshape(parts, modes), padding], axis=0), 0.0)
        south = north * (sign * turn)
        both = jnp.concatenate([north, south], axis=0).astype(BF16)
        sums = nt(both, leg[r])
        cube[pl.ds(pl.multiple_of(r * 8, 8), 8), : sums.shape[1]] = sums[:8]
        cube[pl.ds(pl.multiple_of((HALF + r) * 8, 8), 8), : sums.shape[1]] = sums[8:]

    per_group = group_rows // ROWS_AT_ONCE
    for g in range(groups):
        spec_copy(g).wait()
        leg_copy(g).wait()

        @pl.loop(0, per_group)
        def _(i):
            for k in range(ROWS_AT_ONCE):
                forward_row(g * group_rows + i * ROWS_AT_ONCE + k)

    picker = one_hot(pair_smem, waves)
    for c in range(8):
        if c < parts:
            block = cube[pl.ds(c, 2 * HALF, stride=8), :].astype(BF16)
            flat[pl.ds(c, waves, stride=8), :] = nt(picker, block)
        else:
            flat[pl.ds(c, waves, stride=8), :] = jnp.zeros((waves, SEG), F32)
    send_a[...] = flat[...].reshape(waves, 8, SEG).astype(BF16)

    pl.semaphore_wait(barrier, waves + levels - 2)
    exchange("wave", wave, waves, send_a, recv_a, 0)

    picker_ref[...] = picker
    for r in range(rows):
        own_ref[r : r + 1, :] = jnp.full((1, SEG), order_smem[wave * rows + r].astype(F32))
    gap = jnp.zeros((1, HALF - rows), F32)
    for j in range(chunks):
        first = order_row[:, 2 * j * rows : (2 * j + 1) * rows].astype(F32)
        second = order_row[:, (2 * j + 1) * rows : (2 * j + 2) * rows].astype(F32)
        lanes_ref[j : j + 1, :] = jnp.concatenate([first, gap, second, gap], axis=1)

    pair = pair_smem[wave]
    count = nlon_smem[pair]
    points = jnp.full((1, SEG), count.astype(F32))
    inverse = 1.0 / points
    near_k = lax.broadcasted_iota(jnp.int32, (NEAR, SEG), 0).astype(F32)
    segment = SEG * lax.broadcasted_iota(jnp.int32, (levels, SEG), 0)
    far_k = jnp.concatenate([segment + s for s in range(0, SEG, NEAR)], axis=0).astype(F32)

    @pl.loop(0, chunks)
    def _(j):
        orders = lanes_ref[pl.ds(j, 1), :]
        cosine, sine = unit_circle(near_k * orders, points, inverse)
        near_c[j] = cosine
        near_s[j] = sine
        cosine, sine = unit_circle(far_k * orders, points, inverse)
        both = jnp.concatenate([cosine, -sine], axis=1)
        high = both.astype(BF16).astype(F32)
        far[:, pl.ds(pl.multiple_of(j * 2 * SEG, SEG), 2 * SEG)] = jnp.concatenate(
            [high, both - high], axis=0
        ).astype(BF16)

    arrived(waves, recv_a, 0)

    first_half = lax.broadcasted_iota(jnp.int32, (8, SEG), 1) < HALF

    def turn_chunk(j):
        even = recv_a[2 * j].astype(F32)
        odd = recv_a[2 * j + 1].astype(F32)
        inside = jnp.where(2.0 * lanes_ref[pl.ds(j, 1), :] < points, 1.0, 0.0)
        north = jnp.where(first_half, even, pltpu.roll(odd, HALF, 1)) * inside
        south = jnp.where(first_half, pltpu.roll(even, HALF, 1), odd) * inside
        cosine = near_c[j]
        sine = near_s[j]
        first = pl.ds(pl.multiple_of(j * 2 * SEG, SEG), SEG)
        second = pl.ds(pl.multiple_of(j * 2 * SEG + SEG, SEG), SEG)
        for h, half in enumerate((north, south)):
            for f in range(fields):
                real = half[2 * f : 2 * f + 1]
                imag = half[2 * f + 1 : 2 * f + 2]
                place = slice((h * fields + f) * NEAR, (h * fields + f + 1) * NEAR)
                turned[place, first] = (real * cosine - imag * sine).astype(BF16)
                turned[place, second] = (real * sine + imag * cosine).astype(BF16)

    @pl.loop(0, chunks // CHUNKS_AT_ONCE)
    def _(i):
        for k in range(CHUNKS_AT_ONCE):
            turn_chunk(i * CHUNKS_AT_ONCE + k)

    splits = SEG // NEAR
    quarter = lax.broadcasted_iota(jnp.int32, (levels, SEG), 1) // NEAR

    def swap(blocks):
        results = []
        for p in range(splits):
            result = blocks[p]
            for q, block in enumerate(blocks):
                if q != p:
                    moved = pltpu.roll(block, ((q - p) * NEAR) % SEG, 1)
                    result = jnp.where(quarter == q, moved, result)
            results.append(result)
        return results

    longitude = segment + lax.broadcasted_iota(jnp.int32, (levels, SEG), 1)
    scale = jnp.where(longitude < count, 1.0 / math.sqrt(modes), 0.0)
    sums = nt(turned[...], far[...])
    sums = sums[:, : splits * levels] + sums[:, splits * levels :]
    for first in range(0, parts, splits):
        held_parts = min(splits, parts - first)
        block = sums[first * NEAR : (first + held_parts) * NEAR]
        if held_parts < splits:
            block = jnp.concatenate(
                [block, jnp.zeros((SEG - block.shape[0], block.shape[1]), F32)], axis=0
            )
        block = block.T
        blocks = swap([block[q * levels : (q + 1) * levels] for q in range(splits)])
        for p in range(held_parts):
            flat_p[pl.ds(first + p, levels, stride=8), :] = blocks[p] * scale
    for c in range(parts, 8):
        flat_p[pl.ds(c, levels, stride=8), :] = jnp.zeros((levels, SEG), F32)
    send_f[...] = flat_p[...].reshape(levels, 8, SEG).astype(send_f.dtype)
    exchange("lev", lev, levels, send_f, recv_f, 1)
    arrived(levels, recv_f, 1)

    flat_p[...] = recv_f[...].astype(F32).reshape(levels * 8, SEG)
    level_row = lax.broadcasted_iota(jnp.int32, (levels, levels), 0)
    level_lane = lax.broadcasted_iota(jnp.int32, (levels, levels), 1)
    above = jnp.where(level_lane >= level_row, 1.0, 0.0)
    products = []
    for h in range(2):
        east, north, heat = (
            flat_p[pl.ds(h * fields + f, levels, stride=8), :] for f in range(fields)
        )
        for f, value in enumerate((east, north, heat)):
            grid_ref[h, f] = value
        geopotential = jnp.dot(
            above, heat, precision=lax.Precision.HIGHEST, preferred_element_type=F32
        ) * (1.0 / math.sqrt(levels))
        products += [east * heat, north * heat, east * north + geopotential]
    for hf, value in enumerate(products):
        flat_p[pl.ds(hf, levels, stride=8), :] = value
    send_p[...] = flat_p[...].reshape(levels, 8, SEG).astype(BF16)
    exchange("lev", lev, levels, send_p, recv_p, 2)
    arrived(levels, recv_p, 2)

    flat_p[...] = recv_p[...].astype(F32).reshape(levels * 8, SEG)
    for first in range(0, parts, splits):
        held_parts = min(splits, parts - first)
        blocks = [flat_p[pl.ds(first + p, levels, stride=8), :] for p in range(held_parts)]
        blocks += [jnp.zeros((levels, SEG), F32)] * (splits - held_parts)
        block = jnp.concatenate(swap(blocks), axis=0).T[: held_parts * NEAR]
        turned_p[first * NEAR : (first + held_parts) * NEAR] = jnp.concatenate(
            [block, block], axis=1
        ).astype(BF16)
    total[...] = jnp.zeros_like(total)

    root = lax.rsqrt(points)
    factors = [root * gauss_smem[2 * pair + h] for h in range(2)]

    def return_chunk(j, total):
        cosine = near_c[j]
        sine = near_s[j]
        inner = jnp.dot(
            turned_p[...],
            far[:, pl.ds(pl.multiple_of(j * 2 * SEG, SEG), 2 * SEG)],
            preferred_element_type=F32,
        )
        for h in range(2):
            for f in range(fields):
                place = slice((h * fields + f) * NEAR, (h * fields + f + 1) * NEAR)
                even = inner[place, :SEG]
                odd = inner[place, SEG:]
                real = jnp.sum(even * cosine + odd * sine, axis=0, keepdims=True)
                imag = jnp.sum(odd * cosine - even * sine, axis=0, keepdims=True)
                total[h, 2 * f : 2 * f + 1] = real
                total[h, 2 * f + 1 : 2 * f + 2] = imag
        inside = jnp.where(2.0 * lanes_ref[pl.ds(j, 1), :] < points, 1.0, 0.0)
        north = total[0] * (factors[0] * inside)
        south = total[1] * (factors[1] * inside)
        send_d[2 * j] = jnp.where(first_half, north, pltpu.roll(south, HALF, 1)).astype(BF16)
        send_d[2 * j + 1] = jnp.where(first_half, pltpu.roll(north, HALF, 1), south).astype(BF16)

    @pl.loop(0, chunks // CHUNKS_AT_ONCE)
    def _(i):
        for k in range(CHUNKS_AT_ONCE):
            return_chunk(i * CHUNKS_AT_ONCE + k, total.at[k])

    exchange("wave", wave, waves, send_d, recv_d, 3)
    arrived(waves, recv_d, 3)

    pltpu.make_async_copy(send_d.at[wave], recv_d.at[wave], out_sem.at[0]).wait()

    for index, (size, source) in enumerate(
        ((waves, send_a), (levels, send_f), (levels, send_p), (waves, send_d))
    ):
        left(size, source, index)


def back_kernel(
    waves, fields, rows, modes,
    recv, picker_ref, own_ref, grid, leg,
    grid_hbm, tend_hbm,
    tend, flat, cube, out_sem,
):
    parts = 2 * fields
    groups = out_sem.shape[0] - 1
    group_rows = rows // groups

    def tend_copy(g):
        block = pl.ds(g * group_rows, group_rows)
        return pltpu.make_async_copy(tend.at[block], tend_hbm.at[block], out_sem.at[g])

    grid_copy = pltpu.make_async_copy(grid, grid_hbm, out_sem.at[groups])
    grid_copy.start()
    degree = lax.broadcasted_iota(jnp.int32, (8, modes), 1)
    sign = (1 - 2 * (degree % 2)).astype(F32)
    place = degree.astype(F32)
    outer = math.sqrt(modes / (2 * waves))
    picker = picker_ref[...]
    flat[...] = recv[...].astype(F32).reshape(waves * 8, SEG)
    for c in range(parts):
        block = flat[pl.ds(c, waves, stride=8), :].astype(BF16)
        cube[pl.ds(c, 2 * HALF, stride=8), :] = lax.dot_general(
            block, picker, (((0,), (0,)), ((), ())), preferred_element_type=F32
        )
    for c in range(parts, 8):
        cube[pl.ds(c, 2 * HALF, stride=8), :] = jnp.zeros((2 * HALF, SEG), F32)

    def backward_row(r):
        order = own_ref[pl.ds(r, 1), :1]
        turn = 1.0 - 2.0 * (order - 2.0 * jnp.floor(0.5 * order))
        north = cube[pl.ds(pl.multiple_of(r * 8, 8), 8), :]
        south = cube[pl.ds(pl.multiple_of((HALF + r) * 8, 8), 8), :]
        both = jnp.concatenate([north, south], axis=0)[:, :waves].astype(BF16)
        sums = jnp.dot(both, leg[r], preferred_element_type=F32)
        mixed = (sums[:8] + sums[8:] * (sign * turn)) * outer
        mixed = jnp.where(place >= order, mixed, 0.0).astype(BF16)
        tend[r] = mixed.reshape(4, 2, modes)[:fields]

    for g in range(groups):

        @pl.loop(0, group_rows // ROWS_AT_ONCE)
        def _(i):
            for k in range(ROWS_AT_ONCE):
                backward_row(g * group_rows + i * ROWS_AT_ONCE + k)

        tend_copy(g).start()

    for g in range(groups):
        tend_copy(g).wait()
    grid_copy.wait()


def local(spectral, legendre, gauss, wave_order, pair_order, nlon):
    rows, _, fields, _, modes = spectral.shape
    waves = lax.axis_size("wave")
    levels = lax.axis_size("lev")
    parts = 2 * fields
    spec = jnp.transpose(spectral, (0, 2, 3, 1, 4)).reshape(rows, fields, 2, modes)
    anywhere = pl.BlockSpec(memory_space=pl.ANY)
    groups = max(g for g in (1, 2, 3, 6) if rows % (g * ROWS_AT_ONCE) == 0)
    chunks = waves // 2
    scratch = [
        pltpu.SMEM(wave_order.shape, jnp.int32),
        pltpu.SMEM(pair_order.shape, jnp.int32),
        pltpu.SMEM(nlon.shape, jnp.int32),
        pltpu.SMEM(gauss.shape, F32),
        pltpu.VMEM((1, *wave_order.shape), jnp.int32),
        pltpu.VMEM((chunks, SEG), F32),
        pltpu.VMEM(spec.shape, BF16),
        pltpu.VMEM(legendre.shape, BF16),
        pltpu.VMEM((2 * HALF * 8, SEG), F32),
        pltpu.VMEM((waves * 8, SEG), F32),
        pltpu.VMEM((waves, 8, SEG), BF16),
        pltpu.VMEM((waves, 8, SEG), BF16),
        pltpu.VMEM((chunks, NEAR, SEG), F32),
        pltpu.VMEM((chunks, NEAR, SEG), F32),
        pltpu.VMEM((2 * levels * SEG // NEAR, chunks * 2 * SEG), BF16),
        pltpu.VMEM((parts * NEAR, chunks * 2 * SEG), BF16),
        pltpu.VMEM((levels, 8, SEG), F32),
        pltpu.VMEM((levels, 8, SEG), F32),
        pltpu.VMEM((levels * 8, SEG), F32),
        pltpu.VMEM((levels, 8, SEG), BF16),
        pltpu.VMEM((levels, 8, SEG), BF16),
        pltpu.VMEM((parts * NEAR, 2 * levels * SEG // NEAR), BF16),
        pltpu.VMEM((CHUNKS_AT_ONCE, 2, 8, SEG), F32),
        pltpu.VMEM((waves, 8, SEG), BF16),
        pltpu.SemaphoreType.DMA((5,)),
        pltpu.SemaphoreType.DMA((groups,)),
        pltpu.SemaphoreType.DMA((groups,)),
        pltpu.SemaphoreType.DMA((1,)),
        pltpu.SemaphoreType.DMA((4,)),
        pltpu.SemaphoreType.DMA((4,)),
    ]
    inputs = (wave_order, pair_order, nlon, gauss, spec, legendre)
    grid_shape = jax.ShapeDtypeStruct((2, fields, levels, SEG), F32)
    far_memory = pl.BlockSpec(memory_space=pltpu.HBM)
    vmem = pl.BlockSpec(memory_space=pltpu.VMEM)
    grid, weighted, picker, own = pl.pallas_call(
        functools.partial(kernel, waves, levels, fields, rows, modes),
        out_shape=(
            grid_shape,
            jax.ShapeDtypeStruct((waves, 8, SEG), BF16),
            jax.ShapeDtypeStruct((waves, SEG), BF16),
            jax.ShapeDtypeStruct((rows, SEG), F32),
        ),
        in_specs=[far_memory] * 6,
        out_specs=(vmem, anywhere, vmem, vmem),
        scratch_shapes=scratch,
        compiler_params=pltpu.CompilerParams(
            collective_id=0, has_side_effects=True, vmem_limit_bytes=VMEM_LIMIT
        ),
    )(*(pltpu.with_memory_space_constraint(x, pltpu.HBM) for x in inputs))
    grid, tend = pl.pallas_call(
        functools.partial(back_kernel, waves, fields, rows, modes),
        out_shape=(grid_shape, jax.ShapeDtypeStruct(spec.shape, BF16)),
        in_specs=[vmem] * 5,
        out_specs=(anywhere, anywhere),
        scratch_shapes=[
            pltpu.VMEM(spec.shape, BF16),
            pltpu.VMEM((waves * 8, SEG), F32),
            pltpu.VMEM((2 * HALF * 8, SEG), F32),
            pltpu.SemaphoreType.DMA((groups + 1,)),
        ],
        compiler_params=pltpu.CompilerParams(vmem_limit_bytes=VMEM_LIMIT),
    )(weighted, picker, own, grid, legendre)
    tend = tend.reshape(rows, fields, 1, 2, modes)
    return grid, jnp.transpose(tend, (0, 3, 1, 2, 4))


def solution(mesh):
    in_specs = (P("wave", None, None, "lev", None), P("wave", None, None), P(), P(), P(), P())
    out_specs = (P("wave", None, None, "lev"), P("wave", None, None, "lev", None))
    return jax.shard_map(local, mesh=mesh, in_specs=in_specs, out_specs=out_specs, check_vma=False)
```

time: 68.5 us -> 52.3 us (0.76)
  Pallas kernels: 59.8 us -> 51.6 us
  local copies, waits for them, and re-layouts: 7.76 us -> 0.01 us
    pallas_call x1, Pallas kernels: 59.8 us -> 49.4 us  [local(): pl.pallas_call(functools.partial(kernel, waves, levels, fields, rows, mod...]
    unnamed x5 -> x2, local copies, waits for them, and re-layouts: 3.54 us -> 0.01 us
    pallas_call x0 -> x1, Pallas kernels: none -> 2.16 us  [local(): pl.pallas_call(functools.partial(back_kernel, waves, fields, rows, modes)...]
    slice x1 -> x0, local copies, waits for them, and re-layouts: 1.38 us -> none  [local(): tend = tend[:, :parts].reshape(rows, fields, 1, 2, modes)]
    pad x1 -> x0, local copies, waits for them, and re-layouts: 1.25 us -> none  [local(): spec = jnp.pad(spec, ((0, 0), (0, 8 - parts), (0, 0)))]
    reshape x2 -> x0, local copies, waits for them, and re-layouts: 0.92 us -> none  [the longest x1 0.79 us: local(): lanes = jnp.pad(wave_order.reshape(waves, rows), ((0, 0), (0, HALF - rows)))]
where the time goes in v2:
time: 52.3 us; the launch traced here: 52.2 us
  Pallas kernels  51.6 us (99%)
  between operations  0.66 us (1%)
    pallas_call x1, Pallas kernels, local(): pl.pallas_call(functools.partial(kernel, waves, levels, fields, rows, mod...  49.4 us
    pallas_call x1, Pallas kernels, local(): pl.pallas_call(functools.partial(back_kernel, waves, fields, rows, modes)...  2.16 us

profile of v2, /device:TPU:1, one launch (start us, length us, event | category | flops | bytes accessed | tf_op | source)
XLA Modules:
  0.0 52.2 jit_solution(4124484926529908749)
XLA Ops:
  0.6 0.0 copy-start
  0.6 49.4 %shard_map.77 = (f32[2,3,32,128]{3,2,1,0:T(8,128)S(1)}, bf16[24,8,128]{2,1,0:T(8,128)(2,1)S(1)}, bf16[24,128]{1,0:T(8,128)(2,1)S(1)}, f32[54,128]{1,0:T(8,128)S(1)}) custom-call(s32[1296]{0:T(1024)} %order_hbm.1, s32[24]{0:T(128)} %pair_hbm.1, s32[24]{0:T(128)} %nlon_hbm.1, f32[48]{0:T(128)} %gauss_hbm.1, bf16[54,3,2,1296]{3,2,1,0:T(2,128)(2,1)} %bitcast.10, ...), custom_call_target="tpu_custom_call" | custom-call | tf_op jit(solution)/shard_map/pallas_call | solution.py:431
  50.0 0.0 copy-done
  50.1 2.2 %shard_map.78 = (f32[2,3,32,128]{3,2,1,0:T(8,128)}, bf16[54,3,2,1296]{3,2,1,0:T(2,128)(2,1)}) custom-call(bf16[24,8,128]{2,1,0:T(8,128)(2,1)S(1)} %get-tuple-element.8.recv, bf16[24,128]{1,0:T(8,128)(2,1)S(1)} %get-tuple-element.9.picker_ref, f32[54,128]{1,0:T(8,128)S(1)} %get-tuple-element.10.own_ref, f32[2,3,32,128]{3,2,1,0:T(8,128)S(1)} %get-tuple-element.11.grid, ...), custom_call_target="tpu_custom_call" | custom-call | tf_op jit(solution)/shard_map/pallas_call | solution.py:446
Async XLA Ops:
  0.6 49.4 %copy-start = (bf16[54,24,1296]{2,1,0:T(8,128)(2,1)S(1)}, bf16[54,24,1296]{2,1,0:T(8,128)(2,1)}, u32[]{:S(2)}) copy-start(bf16[54,24,1296]{2,1,0:T(8,128)(2,1)} %leg.1) | copy-start | bytes 10077700

commit v3 on v2

--- a/solution.py
+++ b/solution.py
@@ -16,7 +16,6 @@
 HALF = 64
 NEAR = 32
 ROWS_AT_ONCE = 9
-CHUNKS_AT_ONCE = 2
 SERIES = [(-1.0) ** i * (2.0 * math.pi) ** (2 * i + 1) / math.factorial(2 * i + 1) for i in range(6)]
 
 
@@ -89,18 +88,30 @@
     def wrapped(me, step, count):
         return jnp.where(me + step >= count, me + step - count, me + step)
 
-    def far_first(count):
-        return sorted(range(1, count), key=lambda s: -min(s, count - s))
-
-    for axis, me, size in (("wave", wave, waves), ("lev", lev, levels)):
-        for step in far_first(size):
-            pl.semaphore_signal(
-                barrier, inc=1, device_id={axis: wrapped(me, step, size)}, device_id_type=MESH
-            )
+    def hops(step, count):
+        return min(step, count - step)
+
+    across = 4 if levels % 4 == 0 else 1
+    down = levels // across
+    lev_y = lev // across
+    lev_x = lev % across
+    cores = 2
+    peers = {"wave": [], "lev": []}
+    for step in range(1, waves):
+        peers["wave"].append((hops(step, waves) / cores, wrapped(wave, step, waves)))
+    for dy in range(down):
+        for dx in range(across):
+            if dy or dx:
+                there = wrapped(lev_y, dy, down) * across + wrapped(lev_x, dx, across)
+                peers["lev"].append((hops(dy, down) + hops(dx, across), there))
+    for axis in peers:
+        peers[axis].sort(key=lambda peer: -peer[0])
+    greeted = [(far, axis, there) for axis in peers for far, there in peers[axis]]
+    for _, axis, there in sorted(greeted, key=lambda peer: -peer[0]):
+        pl.semaphore_signal(barrier, inc=1, device_id={axis: there}, device_id_type=MESH)
 
     def exchange(axis, me, count, source, target, index):
-        for step in far_first(count):
-            there = wrapped(me, step, count)
+        for _, there in peers[axis]:
             pltpu.make_async_remote_copy(
                 src_ref=source.at[there],
                 dst_ref=target.at[me],
@@ -134,11 +145,11 @@
         order = order_smem[wave * rows + r]
         turn = (1 - 2 * (order % 2)).astype(F32)
         north = jnp.where(degree >= order, jnp.concatenate([spec[r].astype(F32).reshape(parts, modes), padding], axis=0), 0.0)
-        south = north * (sign * turn)
+        south = north * sign
         both = jnp.concatenate([north, south], axis=0).astype(BF16)
         sums = nt(both, leg[r])
         cube[pl.ds(pl.multiple_of(r * 8, 8), 8), : sums.shape[1]] = sums[:8]
-        cube[pl.ds(pl.multiple_of((HALF + r) * 8, 8), 8), : sums.shape[1]] = sums[8:]
+        cube[pl.ds(pl.multiple_of((HALF + r) * 8, 8), 8), : sums.shape[1]] = sums[8:] * turn
 
     per_group = group_rows // ROWS_AT_ONCE
     for g in range(groups):
@@ -204,8 +215,8 @@
         south = jnp.where(first_half, pltpu.roll(even, HALF, 1), odd) * inside
         cosine = near_c[j]
         sine = near_s[j]
-        first = pl.ds(pl.multiple_of(j * 2 * SEG, SEG), SEG)
-        second = pl.ds(pl.multiple_of(j * 2 * SEG + SEG, SEG), SEG)
+        first = pl.ds(j * 2 * SEG, SEG)
+        second = pl.ds(j * 2 * SEG + SEG, SEG)
         for h, half in enumerate((north, south)):
             for f in range(fields):
                 real = half[2 * f : 2 * f + 1]
@@ -214,10 +225,8 @@
                 turned[place, first] = (real * cosine - imag * sine).astype(BF16)
                 turned[place, second] = (real * sine + imag * cosine).astype(BF16)
 
-    @pl.loop(0, chunks // CHUNKS_AT_ONCE)
-    def _(i):
-        for k in range(CHUNKS_AT_ONCE):
-            turn_chunk(i * CHUNKS_AT_ONCE + k)
+    for j in range(chunks):
+        turn_chunk(j)
 
     splits = SEG // NEAR
     quarter = lax.broadcasted_iota(jnp.int32, (levels, SEG), 1) // NEAR
@@ -294,7 +303,7 @@
         sine = near_s[j]
         inner = jnp.dot(
             turned_p[...],
-            far[:, pl.ds(pl.multiple_of(j * 2 * SEG, SEG), 2 * SEG)],
+            far[:, pl.ds(j * 2 * SEG, 2 * SEG)],
             preferred_element_type=F32,
         )
         for h in range(2):
@@ -312,10 +321,8 @@
         send_d[2 * j] = jnp.where(first_half, north, pltpu.roll(south, HALF, 1)).astype(BF16)
         send_d[2 * j + 1] = jnp.where(first_half, pltpu.roll(north, HALF, 1), south).astype(BF16)
 
-    @pl.loop(0, chunks // CHUNKS_AT_ONCE)
-    def _(i):
-        for k in range(CHUNKS_AT_ONCE):
-            return_chunk(i * CHUNKS_AT_ONCE + k, total.at[k])
+    for j in range(chunks):
+        return_chunk(j, total.at[j])
 
     exchange("wave", wave, waves, send_d, recv_d, 3)
     arrived(waves, recv_d, 3)
@@ -362,10 +369,10 @@
         order = own_ref[pl.ds(r, 1), :1]
         turn = 1.0 - 2.0 * (order - 2.0 * jnp.floor(0.5 * order))
         north = cube[pl.ds(pl.multiple_of(r * 8, 8), 8), :]
-        south = cube[pl.ds(pl.multiple_of((HALF + r) * 8, 8), 8), :]
+        south = cube[pl.ds(pl.multiple_of((HALF + r) * 8, 8), 8), :] * turn
         both = jnp.concatenate([north, south], axis=0)[:, :waves].astype(BF16)
         sums = jnp.dot(both, leg[r], preferred_element_type=F32)
-        mixed = (sums[:8] + sums[8:] * (sign * turn)) * outer
+        mixed = (sums[:8] + sums[8:] * sign) * outer
         mixed = jnp.where(place >= order, mixed, 0.0).astype(BF16)
         tend[r] = mixed.reshape(4, 2, modes)[:fields]
 
@@ -409,13 +416,13 @@
         pltpu.VMEM((chunks, NEAR, SEG), F32),
         pltpu.VMEM((2 * levels * SEG // NEAR, chunks * 2 * SEG), BF16),
         pltpu.VMEM((parts * NEAR, chunks * 2 * SEG), BF16),
-        pltpu.VMEM((levels, 8, SEG), F32),
-        pltpu.VMEM((levels, 8, SEG), F32),
+        pltpu.VMEM((levels, 8, SEG), BF16),
+        pltpu.VMEM((levels, 8, SEG), BF16),
         pltpu.VMEM((levels * 8, SEG), F32),
         pltpu.VMEM((levels, 8, SEG), BF16),
         pltpu.VMEM((levels, 8, SEG), BF16),
         pltpu.VMEM((parts * NEAR, 2 * levels * SEG // NEAR), BF16),
-        pltpu.VMEM((CHUNKS_AT_ONCE, 2, 8, SEG), F32),
+        pltpu.VMEM((chunks, 2, 8, SEG), F32),
         pltpu.VMEM((waves, 8, SEG), BF16),
         pltpu.SemaphoreType.DMA((5,)),
         pltpu.SemaphoreType.DMA((groups,)),

time: 52.3 us -> 49.2 us (0.941)
  Pallas kernels: 51.6 us -> 48.4 us
    pallas_call x1, Pallas kernels: 49.4 us -> 46.6 us  [local(): pl.pallas_call(functools.partial(kernel, waves, levels, fields, rows, mod...]
where the time goes in v3:
time: 49.2 us; the launch traced here: 49.1 us
  Pallas kernels  48.4 us (98%)
  between operations  0.66 us (1%)
    pallas_call x1, Pallas kernels, local(): pl.pallas_call(functools.partial(kernel, waves, levels, fields, rows, mod...  46.6 us
    pallas_call x1, Pallas kernels, local(): pl.pallas_call(functools.partial(back_kernel, waves, fields, rows, modes)...  1.89 us

profile of v3, /device:TPU:1, one launch (start us, length us, event | category | flops | bytes accessed | tf_op | source)
XLA Modules:
  0.0 49.1 jit_solution(6992196810690402811)
XLA Ops:
  0.6 0.0 copy-start
  0.6 46.6 %shard_map.77 = (f32[2,3,32,128]{3,2,1,0:T(8,128)S(1)}, bf16[24,8,128]{2,1,0:T(8,128)(2,1)S(1)}, bf16[24,128]{1,0:T(8,128)(2,1)S(1)}, f32[54,128]{1,0:T(8,128)S(1)}) custom-call(s32[1296]{0:T(1024)} %order_hbm.1, s32[24]{0:T(128)} %pair_hbm.1, s32[24]{0:T(128)} %nlon_hbm.1, f32[48]{0:T(128)} %gauss_hbm.1, bf16[54,3,2,1296]{3,2,1,0:T(2,128)(2,1)} %bitcast.10, ...), custom_call_target="tpu_custom_call" | custom-call | tf_op jit(solution)/shard_map/pallas_call | solution.py:438
  47.2 0.0 copy-done
  47.2 1.9 %shard_map.78 = (f32[2,3,32,128]{3,2,1,0:T(8,128)}, bf16[54,3,2,1296]{3,2,1,0:T(2,128)(2,1)}) custom-call(bf16[24,8,128]{2,1,0:T(8,128)(2,1)S(1)} %get-tuple-element.8.recv, bf16[24,128]{1,0:T(8,128)(2,1)S(1)} %get-tuple-element.9.picker_ref, f32[54,128]{1,0:T(8,128)S(1)} %get-tuple-element.10.own_ref, f32[2,3,32,128]{3,2,1,0:T(8,128)S(1)} %get-tuple-element.11.grid, ...), custom_call_target="tpu_custom_call" | custom-call | tf_op jit(solution)/shard_map/pallas_call | solution.py:453
Async XLA Ops:
  0.6 46.6 %copy-start = (bf16[54,24,1296]{2,1,0:T(8,128)(2,1)S(1)}, bf16[54,24,1296]{2,1,0:T(8,128)(2,1)}, u32[]{:S(2)}) copy-start(bf16[54,24,1296]{2,1,0:T(8,128)(2,1)} %leg.1) | copy-start | bytes 10077700

commit v4 on v3

--- a/solution.py
+++ b/solution.py
@@ -49,9 +49,9 @@
 def kernel(
     waves, levels, fields, rows, modes,
     order_hbm, pair_hbm, nlon_hbm, gauss_hbm, spec_hbm, leg_hbm,
-    grid_ref, recv_d, picker_ref, own_ref,
+    grid_ref, recv_d, picker_ref, own_ref, leg,
     order_smem, pair_smem, nlon_smem, gauss_smem, order_row, lanes_ref, spec,
-    leg, cube, flat, send_a, recv_a, near_c, near_s, far, turned,
+    cube, flat, send_a, recv_a, near_c, near_s, far, turned,
     send_f, recv_f, flat_p, send_p, recv_p, turned_p, total, send_d,
     small_sem, leg_sem, spec_sem, out_sem, send_sem, recv_sem,
 ):
@@ -68,7 +68,9 @@
 
     def spec_copy(g):
         block = pl.ds(g * group_rows, group_rows)
-        return pltpu.make_async_copy(spec_hbm.at[block], spec.at[block], spec_sem.at[g])
+        return pltpu.make_async_copy(
+            spec_hbm.at[block], spec.at[block, pl.ds(0, fields)], spec_sem.at[g]
+        )
 
     small = [
         pltpu.make_async_copy(order_hbm, order_smem, small_sem.at[0]),
@@ -138,13 +140,12 @@
     for copy in small:
         copy.wait()
     degree = lax.broadcasted_iota(jnp.int32, (8, modes), 1)
-    padding = jnp.zeros((8 - parts, modes), F32)
     sign = (1 - 2 * (degree % 2)).astype(F32)
 
     def forward_row(r):
         order = order_smem[wave * rows + r]
         turn = (1 - 2 * (order % 2)).astype(F32)
-        north = jnp.where(degree >= order, jnp.concatenate([spec[r].astype(F32).reshape(parts, modes), padding], axis=0), 0.0)
+        north = jnp.where(degree >= order, spec[r].reshape(8, modes).astype(F32), 0.0)
         south = north * sign
         both = jnp.concatenate([north, south], axis=0).astype(BF16)
         sums = nt(both, leg[r])
@@ -347,7 +348,9 @@
 
     def tend_copy(g):
         block = pl.ds(g * group_rows, group_rows)
-        return pltpu.make_async_copy(tend.at[block], tend_hbm.at[block], out_sem.at[g])
+        return pltpu.make_async_copy(
+            tend.at[block, pl.ds(0, fields)], tend_hbm.at[block], out_sem.at[g]
+        )
 
     grid_copy = pltpu.make_async_copy(grid, grid_hbm, out_sem.at[groups])
     grid_copy.start()
@@ -374,7 +377,7 @@
         sums = jnp.dot(both, leg[r], preferred_element_type=F32)
         mixed = (sums[:8] + sums[8:] * sign) * outer
         mixed = jnp.where(place >= order, mixed, 0.0).astype(BF16)
-        tend[r] = mixed.reshape(4, 2, modes)[:fields]
+        tend[r] = mixed.reshape(4, 2, modes)
 
     for g in range(groups):
 
@@ -406,8 +409,7 @@
         pltpu.SMEM(gauss.shape, F32),
         pltpu.VMEM((1, *wave_order.shape), jnp.int32),
         pltpu.VMEM((chunks, SEG), F32),
-        pltpu.VMEM(spec.shape, BF16),
-        pltpu.VMEM(legendre.shape, BF16),
+        pltpu.VMEM((rows, 4, 2, modes), BF16),
         pltpu.VMEM((2 * HALF * 8, SEG), F32),
         pltpu.VMEM((waves * 8, SEG), F32),
         pltpu.VMEM((waves, 8, SEG), BF16),
@@ -435,16 +437,17 @@
     grid_shape = jax.ShapeDtypeStruct((2, fields, levels, SEG), F32)
     far_memory = pl.BlockSpec(memory_space=pltpu.HBM)
     vmem = pl.BlockSpec(memory_space=pltpu.VMEM)
-    grid, weighted, picker, own = pl.pallas_call(
+    grid, weighted, picker, own, table = pl.pallas_call(
         functools.partial(kernel, waves, levels, fields, rows, modes),
         out_shape=(
             grid_shape,
             jax.ShapeDtypeStruct((waves, 8, SEG), BF16),
             jax.ShapeDtypeStruct((waves, SEG), BF16),
             jax.ShapeDtypeStruct((rows, SEG), F32),
+            jax.ShapeDtypeStruct(legendre.shape, BF16),
         ),
         in_specs=[far_memory] * 6,
-        out_specs=(vmem, anywhere, vmem, vmem),
+        out_specs=(vmem, anywhere, vmem, vmem, vmem),
         scratch_shapes=scratch,
         compiler_params=pltpu.CompilerParams(
             collective_id=0, has_side_effects=True, vmem_limit_bytes=VMEM_LIMIT
@@ -456,13 +459,13 @@
         in_specs=[vmem] * 5,
         out_specs=(anywhere, anywhere),
         scratch_shapes=[
-            pltpu.VMEM(spec.shape, BF16),
+            pltpu.VMEM((rows, 4, 2, modes), BF16),
             pltpu.VMEM((waves * 8, SEG), F32),
             pltpu.VMEM((2 * HALF * 8, SEG), F32),
             pltpu.SemaphoreType.DMA((groups + 1,)),
         ],
         compiler_params=pltpu.CompilerParams(vmem_limit_bytes=VMEM_LIMIT),
-    )(weighted, picker, own, grid, legendre)
+    )(weighted, picker, own, grid, table)
     tend = tend.reshape(rows, fields, 1, 2, modes)
     return grid, jnp.transpose(tend, (0, 3, 1, 2, 4))
 

time: 49.2 us -> 49.2 us (level)
  no operation moved by 1% of the time
where the time goes in v4:
time: 49.2 us; the launch traced here: 49 us
  Pallas kernels  48.4 us (98%)
  between operations  0.64 us (1%)
    pallas_call x1, Pallas kernels, local(): pl.pallas_call(functools.partial(kernel, waves, levels, fields, rows, mod...  46.5 us
    pallas_call x1, Pallas kernels, local(): pl.pallas_call(functools.partial(back_kernel, waves, fields, rows, modes)...  1.92 us

profile of v4, /device:TPU:1, one launch (start us, length us, event | category | flops | bytes accessed | tf_op | source)
XLA Modules:
  0.0 49.0 jit_solution(9027311048202740220)
XLA Ops:
  0.6 46.5 %shard_map.77 = (f32[2,3,32,128]{3,2,1,0:T(8,128)S(1)}, bf16[24,8,128]{2,1,0:T(8,128)(2,1)S(1)}, bf16[24,128]{1,0:T(8,128)(2,1)S(1)}, f32[54,128]{1,0:T(8,128)S(1)}, bf16[54,24,1296]{2,1,0:T(8,128)(2,1)S(1)}) custom-call(s32[1296]{0:T(1024)} %order_hbm.1, s32[24]{0:T(128)} %pair_hbm.1, s32[24]{0:T(128)} %nlon_hbm.1, f32[48]{0:T(128)} %gauss_hbm.1, ...), custom_call_target="tpu_custom_call" | custom-call | tf_op jit(solution)/shard_map/pallas_call | solution.py:440
  47.1 1.9 %shard_map.78 = (f32[2,3,32,128]{3,2,1,0:T(8,128)}, bf16[54,3,2,1296]{3,2,1,0:T(2,128)(2,1)}) custom-call(bf16[24,8,128]{2,1,0:T(8,128)(2,1)S(1)} %get-tuple-element.9.recv, bf16[24,128]{1,0:T(8,128)(2,1)S(1)} %get-tuple-element.10.picker_ref, f32[54,128]{1,0:T(8,128)S(1)} %get-tuple-element.11.own_ref, f32[2,3,32,128]{3,2,1,0:T(8,128)S(1)} %get-tuple-element.12.grid, ...), custom_call_target="tpu_custom_call" | custom-call | tf_op jit(solution)/shard_map/pallas_call | solution.py:456
